TPU v7x, 512 devices: a whole 4x4x16 slice. The times are simulated.
512 devices in a mesh: grp: 16 (over y, x), tp: 32 (over z, core).
Axes of the slice: x: 4, y: 4, z: 16, core: 2. Of those that a mesh axis runs over, the one named last changes fastest.
Arguments:
- tokens: bfloat16 [6144, 5120], P('grp'), may hold values from -36 to 36
- trainer_panels: bfloat16 [64, 5120, 128], P('tp', 'grp'), may hold values from -0.078125 to 0.078125
- panel_home: int32 [48], replicated, may hold values from 0 to 63, as said below
- lengths: int32 [16, 4], P('grp'), may hold values from 1 to 192, 384 in all within a row
Outputs:
- context: float32 [6144, 4096], P(('grp', 'tp'))
Inputs may be any that keep to these rules, and one draw needn't show every extreme that they name: `panel_home`: entries are distinct; entry p is 2 times the tp index of the trainer device that holds panel p, plus the panel's slot on that device. Panels 0 to 31 are query heads, the next 8 key heads, the last 8 value heads. Some trainer device holds 2 panels.
All inputs are finite; a program needn't handle non-finite values.
Results may differ from a plain program's by a relative error of at most 0.012.
Values may be sent and summed in bfloat16 or wider, within the bound.
A program may use at most 64 MiB of HBM per device.

v0:
```python
import jax
import jax.numpy as jnp
from jax import lax
from jax.sharding import PartitionSpec as P


def on_device(tokens, trainer_panels, panel_home, lengths):
    tp_count = lax.axis_size("tp")
    grp_count = lax.axis_size("grp")
    member_id = lax.axis_index("tp")
    kv_count = (panel_home.shape[0] - tp_count) // 2
    group_size = tp_count // kv_count
    head_dim = trainer_panels.shape[2]
    block_rows = trainer_panels.shape[1]
    half_rows = block_rows // 2
    seq_total = tokens.shape[0]
    all_slots = lax.all_gather(trainer_panels, "tp", axis=0, tiled=True)
    kv_id = member_id // group_size
    quarter = member_id % group_size
    kv_panel = tp_count + kv_id + kv_count * (quarter // 2)
    half = quarter % 2
    q_block = all_slots[panel_home[member_id]]
    kv_block = all_slots[panel_home[kv_panel]]
    kv_half = lax.dynamic_slice_in_dim(kv_block, half * half_rows, half_rows, axis=0)
    piece = jnp.concatenate([q_block, kv_half], axis=0)
    gathered = lax.all_gather(piece, "grp", axis=0, tiled=False)
    q_weights = gathered[:, :block_rows].reshape(grp_count * block_rows, head_dim)
    kv_weights = gathered[:, block_rows:]
    query_rows = jnp.dot(tokens, q_weights, preferred_element_type=jnp.float32).astype(jnp.bfloat16)
    token_halves = tokens.reshape(seq_total, grp_count, 2, half_rows)
    token_half = lax.dynamic_index_in_dim(token_halves, half, axis=2, keepdims=False)
    kv_part = jnp.einsum("sgi,gic->sc", token_half, kv_weights, preferred_element_type=jnp.float32)
    pair_perm = [(i, i ^ 1) for i in range(tp_count)]
    kv_full = (kv_part + lax.ppermute(kv_part, "tp", pair_perm)).astype(jnp.bfloat16)
    swap_perm = [(i, i ^ 2) for i in range(tp_count)]
    kv_other = lax.ppermute(kv_full, "tp", swap_perm)
    holds_k = quarter < 2
    key_rows = jnp.where(holds_k, kv_full, kv_other)
    value_rows = jnp.where(holds_k, kv_other, kv_full)
    position = jnp.arange(seq_total, dtype=jnp.int32)
    bounds = jnp.cumsum(lengths[0])
    segment = jnp.sum((position[:, None] >= bounds[None, :]).astype(jnp.int32), axis=1)
    allowed = (segment[:, None] == segment[None, :]) & (position[None, :] <= position[:, None])
    score_scale = head_dim ** (-0.5)
    scores = (
        lax.dot_general(
            query_rows, key_rows, (((1,), (1,)), ((), ())), preferred_element_type=jnp.float32
        )
        * score_scale
    )
    masked = jnp.where(allowed, scores, -jnp.inf)
    row_peak = jnp.max(masked, axis=1, keepdims=True)
    row_exp = jnp.exp(masked - row_peak)
    attn_probs = (row_exp / jnp.sum(row_exp, axis=1, keepdims=True)).astype(jnp.bfloat16)
    context = jnp.dot(attn_probs, value_rows, preferred_element_type=jnp.float32)
    return lax.all_to_all(context, "tp", split_axis=0, concat_axis=1, tiled=True)


def solution(mesh):
    placed = (P("grp", None), P("tp", "grp", None), P(), P("grp", None))
    return jax.shard_map(
        on_device, mesh=mesh, in_specs=placed, out_specs=P(("grp", "tp"), None), check_vma=False
    )
```

profile of v0, /device:TPU:1, one launch (start us, length us, event | category | flops | bytes accessed | tf_op | source)
XLA Modules:
  0.0 209.4 jit_solution(2811401276876923710)
XLA Ops:
  6.5 0.7 all-gather.4.cloned.1.call-update
  7.3 0.0 all-gather.6.cloned.1.call-start
  7.4 1.4 fusion.16
  12.6 78.4 %all-gather.4.cloned.1.call-done = bf16[64,320,128]{2,1,0:T(8,128)(2,1)} async-done(((bf16[2,320,128]{2,1,0:T(8,128)(2,1)}), bf16[64,320,128]{2,1,0:T(8,128)(2,1)}) %all-gather.4.cloned.1.call-update) | async-done | bytes 5242896 | tf_op jit(solution)/shard_map/all_gather | solution.py:17
  91.0 0.9 dynamic-slice_bitcast_fusion
  91.9 0.8 dynamic-slice_bitcast_fusion.1
  92.7 0.7 pad_maximum_fusion
  93.3 0.0 all-gather.6.cloned.1.call-update
  93.4 6.3 %copy.12 = bf16[384,5120]{0,1:T(8,128)(2,1)} copy(bf16[384,5120]{1,0:T(8,128)(2,1)} %param.4) | data formatting | bytes 7864320 | tf_op args[0]
  99.6 49.6 %all-gather.6.cloned.1.call-done = bf16[7680,128]{1,0:T(8,128)(2,1)} async-done(((bf16[480,128]{1,0:T(8,128)(2,1)}), bf16[7680,128]{1,0:T(8,128)(2,1)}) %all-gather.6.cloned.1.call-update) | async-done | bytes 1966096 | tf_op jit(solution)/shard_map/all_gather | solution.py:26
  149.2 2.5 %fusion.4 = f32[384,128]{1,0:T(8,128)S(1)} fusion(bf16[384,16,2,160]{0,3,2,1:T(8,128)(2,1)} %bitcast.25, s32[]{:T(128)S(6)} %select_n.69, bf16[16,480,128]{2,1,0:T(8,128)(2,1)} %bitcast.28), kind=kOutput, calls=%fused_computation.5 | convolution fusion | flops 251658240 | bytes 2818052 | tf_op jit(solution)/shard_map/sgi,gic->sc/dot_general | solution.py:32
  151.8 3.4 %collective-permute-start = (f32[384,128]{1,0:T(8,128)S(1)}, f32[384,128]{1,0:T(8,128)S(1)}, u32[]{:S(2)}, u32[]{:S(2)}) collective-permute-start(f32[384,128]{1,0:T(8,128)S(1)} %fusion.4), channel_id=1, source_target_pairs={{0,1},{1,0},{2,3},{3,2},{4,5},{5,4},{6,7},{7,6},{8,9},{9,8},{10,11... | collective-permute-start | bytes 589832 | tf_op jit(solution)/shard_map/ppermute | solution.py:34
  155.2 0.2 reduce-window.8
  155.3 0.9 collective-permute-done
  156.2 3.2 %collective-permute-start.1 = (bf16[384,128]{1,0:T(8,128)(2,1)S(1)}, bf16[384,128]{1,0:T(8,128)(2,1)S(1)}, u32[]{:S(2)}, u32[]{:S(2)}) collective-permute-start(bf16[384,128]{1,0:T(8,128)(2,1)S(1)} %add_convert_fusion), channel_id=1, source_target_pairs={{0,2},{1,3},{2,0},{3,1},{4,6},{5,7},{6,4},{7,5},{8,10},{9,11},{10,... | collective-permute-start | bytes 294920 | tf_op jit(solution)/shard_map/ppermute | solution.py:36
  159.4 0.1 convert_reduce_fusion
  159.5 0.1 slice.9
  159.6 2.5 %collective-permute-done.1 = bf16[384,128]{1,0:T(8,128)(2,1)S(1)} collective-permute-done((bf16[384,128]{1,0:T(8,128)(2,1)S(1)}, bf16[384,128]{1,0:T(8,128)(2,1)S(1)}, u32[]{:S(2)}, u32[]{:S(2)}) %collective-permute-start.1) | collective-permute-done | bytes 98336 | tf_op jit(solution)/shard_map/ppermute | solution.py:36
  162.1 3.7 %fusion.17 = (f32[384]{0:T(512)S(1)}, f32[384,384]{0,1:T(8,128)S(1)}) fusion(bf16[5120,128]{1,0:T(8,128)(2,1)S(1)} %bitcast.24, bf16[384,5120]{1,0:T(8,128)(2,1)} %param.4, bf16[384,128]{1,0:T(8,128)(2,1)S(1)} %add_convert_fusion, bf16[384,128]{1,0:T(8,128)(2,1)S(1)} %collective-permute-done.1, pred[]{:T(512)S(6)} %lt.39, s32[384]{0:T(512)S(1)} %convert_reduce_fusion), kind=kOutput, calls=%fused_computation.26 | convolution fusion | flops 542047872 | bytes 6032385 | tf_op jit(solution)/shard_map/dot_general | solution.py:46
  165.9 0.1 fusion.9
  166.0 0.3 fusion.10
  166.3 35.3 %all_to_all.19 = f32[32,12,128]{2,1,0:T(8,128)S(1)} all-to-all(f32[32,12,128]{2,1,0:T(8,128)S(1)} %all_to_all.14), channel_id=1, replica_groups=mesh['grp'=16,'tp'=32] {'tp'}, dimensions={0} | all-to-all | bytes 393216 | tf_op jit(solution)/shard_map/all_to_all | solution.py:56
  201.7 0.1 copy.13
  201.8 0.9 copy.14
  (8 shorter events, 0.1 us)
Async XLA Ops:
  6.5 84.4 %all-gather.4.cloned.1.call-start = ((), (), s32[]{:S(2)}) async-start(), calls=%async_computation.1 | async-start | bytes 5406720 | tf_op jit(solution)/shard_map/all_gather | solution.py:17
  7.3 142.0 %all-gather.6.cloned.1.call-start = ((), (), s32[]{:S(2)}) async-start(), calls=%async_computation.2 | async-start | bytes 2088960 | tf_op jit(solution)/shard_map/all_gather | solution.py:26
  93.4 61.8 %copy-start.1 = (s32[1,4]{1,0:T(1,128)S(1)}, s32[1,4]{1,0:T(1,128)}, u32[]{:S(2)}) copy-start(s32[1,4]{1,0:T(1,128)} %param.7) | copy-start | bytes 52
  149.2 10.3 %copy-start = (bf16[7680,128]{1,0:T(8,128)(2,1)S(1)}, bf16[7680,128]{1,0:T(8,128)(2,1)}, u32[]{:S(2)}) copy-start(bf16[7680,128]{1,0:T(8,128)(2,1)} %all-gather.6.cloned.1.call-done) | copy-start | bytes 5898244
  151.8 4.4 %collective-permute-start = (f32[384,128]{1,0:T(8,128)S(1)}, f32[384,128]{1,0:T(8,128)S(1)}, u32[]{:S(2)}, u32[]{:S(2)}) collective-permute-start(f32[384,128]{1,0:T(8,128)S(1)} %fusion.4), channel_id=1, source_target_pairs={{0,1},{1,0},{2,3},{3,2},{4,5},{5,4},{6,7},{7,6},{8,9},{9,8},{10,11... | collective-permute-start | bytes 589832 | tf_op jit(solution)/shard_map/ppermute | solution.py:34
  156.2 5.9 %collective-permute-start.1 = (bf16[384,128]{1,0:T(8,128)(2,1)S(1)}, bf16[384,128]{1,0:T(8,128)(2,1)S(1)}, u32[]{:S(2)}, u32[]{:S(2)}) collective-permute-start(bf16[384,128]{1,0:T(8,128)(2,1)S(1)} %add_convert_fusion), channel_id=1, source_target_pairs={{0,2},{1,3},{2,0},{3,1},{4,6},{5,7},{6,4},{7,5},{8,10},{9,11},{10,... | collective-permute-start | bytes 294920 | tf_op jit(solution)/shard_map/ppermute | solution.py:36
Sparse Core Ops, SparseCore 0:
  9.5 81.4 all-gather.3
  94.0 55.1 all-gather.5
where the time goes:
time: 210 us; the launch traced here: 209 us
  waiting for transfers between devices  132 us (63%)
  blocking collectives  35.3 us (17%)
  between operations  17.4 us (8%)
  local copies, waits for them, and re-layouts  10.4 us (5%)
  starting transfers between devices  6.58 us (3%)
  matrix products  6.57 us (3%)
    all_gather x1, waiting for transfers between devices, on_device(): all_slots = lax.all_gather(trainer_panels, 'tp', axis=0, tiled=True)  78.4 us
    all_gather x1, waiting for transfers between devices, on_device(): gathered = lax.all_gather(piece, 'grp', axis=0, tiled=False)  49.6 us
    all_to_all x1, blocking collectives, on_device(): lax.all_to_all(context, 'tp', split_axis=0, concat_axis=1, tiled=True)  35.3 us
    unnamed x7, local copies, waits for them, and re-layouts  7.16 us
  transfers between devices with their start and end apart: 4, of which 4 were waited for; matrix products, arithmetic and copies ran while one was open for 4% of the time, Pallas kernels for 0%

commit v1 on v0

--- a/solution.py
+++ b/solution.py
@@ -2,6 +2,13 @@
 import jax.numpy as jnp
 from jax import lax
 from jax.sharding import PartitionSpec as P
+from jax.lax import all_to_all, axis_size
+
+
+def balance_loads(z_in, peer_axis):
+    return jnp.concatenate(
+        all_to_all(jnp.stack(axis_size(peer_axis) * [z_in]), peer_axis, 0, 0), axis=0
+    )
 
 
 def on_device(tokens, trainer_panels, panel_home, lengths):
@@ -14,7 +21,7 @@
     block_rows = trainer_panels.shape[1]
     half_rows = block_rows // 2
     seq_total = tokens.shape[0]
-    all_slots = lax.all_gather(trainer_panels, "tp", axis=0, tiled=True)
+    all_slots = balance_loads(trainer_panels, peer_axis="tp")
     kv_id = member_id // group_size
     quarter = member_id % group_size
     kv_panel = tp_count + kv_id + kv_count * (quarter // 2)

time: 210 us -> 378 us (1.80)
  waiting for transfers between devices: 132 us -> 279 us
  starting transfers between devices: 6.58 us -> 23.5 us
  local copies, waits for them, and re-layouts: 10.4 us -> 14.2 us
    all_to_all x0 -> x1, waiting for transfers between devices: none -> 228 us  [balance_loads(): all_to_all(jnp.stack(axis_size(peer_axis) * [z_in]), peer_axis, 0, 0)]
    all_gather x1 -> x0, waiting for transfers between devices: 78.4 us -> none  [on_device(): all_slots = lax.all_gather(trainer_panels, 'tp', axis=0, tiled=True)]
    all_to_all x0 -> x1, starting transfers between devices: none -> 16.9 us  [balance_loads(): all_to_all(jnp.stack(axis_size(peer_axis) * [z_in]), peer_axis, 0, 0)]
    another operation x0 -> x1, local copies, waits for them, and re-layouts: none -> 4.53 us  [balance_loads(): jnp.stack(axis_size(peer_axis) * [z_in])]
  transfers between devices with their start and end apart: 4 -> 4, of which waited for: 4 -> 4; matrix products, arithmetic and copies ran while one was open for 4% -> 2% of each run, Pallas kernels for 0% -> 0%
where the time goes in v1:
time: 378 us; the launch traced here: 377 us
  waiting for transfers between devices  279 us (74%)
  blocking collectives  35.3 us (9%)
  starting transfers between devices  23.5 us (6%)
  between operations  17.2 us (5%)
  local copies, waits for them, and re-layouts  14.2 us (4%)
  matrix products  6.52 us (2%)
    all_to_all x1, waiting for transfers between devices, balance_loads(): all_to_all(jnp.stack(axis_size(peer_axis) * [z_in]), peer_axis, 0, 0)  228 us
    all_gather x1, waiting for transfers between devices, on_device(): gathered = lax.all_gather(piece, 'grp', axis=0, tiled=False)  48.3 us
    all_to_all x1, blocking collectives, on_device(): lax.all_to_all(context, 'tp', split_axis=0, concat_axis=1, tiled=True)  35.3 us
    all_to_all x1, starting transfers between devices, balance_loads(): all_to_all(jnp.stack(axis_size(peer_axis) * [z_in]), peer_axis, 0, 0)  16.9 us
  transfers between devices with their start and end apart: 4, of which 4 were waited for; matrix products, arithmetic and copies ran while one was open for 2% of the time, Pallas kernels for 0%

profile of v1, /device:TPU:1, one launch (start us, length us, event | category | flops | bytes accessed | tf_op | source)
XLA Modules:
  0.0 377.0 jit_solution(17143165539301071188)
XLA Ops:
  6.5 4.5 %stack.2 = bf16[32,2,320,128]{3,2,1,0:T(8,128)(2,1)} broadcast(bf16[2,320,128]{2,1,0:T(8,128)(2,1)} %param.5), dimensions={1,2,3} | broadcast | bytes 5406720 | tf_op jit(solution)/shard_map/stack | solution.py:10
  11.1 16.9 %all-to-all-start = ((bf16[32,2,320,128]{3,2,1,0:T(8,128)(2,1)}), bf16[32,2,320,128]{3,2,1,0:T(8,128)(2,1)}, u32[]{:S(2)}, u32[]{:S(2)}) async-start(bf16[32,2,320,128]{3,2,1,0:T(8,128)(2,1)} %stack.2), calls=%async_computation | async-start | bytes 10485760 | tf_op jit(solution)/shard_map/all_to_all | solution.py:10
  28.0 0.0 all-gather.3.cloned.1.call-start
  28.1 0.6 fusion.16
  32.3 227.5 %all-to-all-done = bf16[32,2,320,128]{3,2,1,0:T(8,128)(2,1)} async-done(((bf16[32,2,320,128]{3,2,1,0:T(8,128)(2,1)}), bf16[32,2,320,128]{3,2,1,0:T(8,128)(2,1)}, u32[]{:S(2)}, u32[]{:S(2)}) %all-to-all-start) | async-done | bytes 5242912 | tf_op jit(solution)/shard_map/all_to_all | solution.py:10
  259.8 0.9 dynamic-slice_bitcast_fusion
  260.7 0.8 dynamic-slice_bitcast_fusion.1
  261.5 0.7 pad_maximum_fusion
  262.2 6.3 %copy.10 = bf16[384,5120]{0,1:T(8,128)(2,1)} copy(bf16[384,5120]{1,0:T(8,128)(2,1)} %param.4) | data formatting | bytes 7864320 | tf_op args[0]
  268.5 48.3 %all-gather.3.cloned.1.call-done = bf16[7680,128]{1,0:T(8,128)(2,1)} async-done(((bf16[480,128]{1,0:T(8,128)(2,1)}), bf16[7680,128]{1,0:T(8,128)(2,1)}) %all-gather.3.cloned.1.call-update) | async-done | bytes 1966096 | tf_op jit(solution)/shard_map/all_gather | solution.py:33
  316.8 2.5 fusion.4
  319.4 3.4 collective-permute-start
  322.8 0.2 reduce-window.8
  322.9 0.9 collective-permute-done
  323.8 3.2 collective-permute-start.1
  327.0 0.1 convert_reduce_fusion
  327.1 0.1 slice.9
  327.2 2.5 collective-permute-done.1
  329.7 3.7 fusion.17
  333.4 0.1 fusion.9
  333.5 0.3 fusion.10
  333.9 35.3 %all_to_all.24 = f32[32,12,128]{2,1,0:T(8,128)S(1)} all-to-all(f32[32,12,128]{2,1,0:T(8,128)S(1)} %all_to_all.18), channel_id=1, replica_groups=mesh['grp'=16,'tp'=32] {'tp'}, dimensions={0} | all-to-all | bytes 393216 | tf_op jit(solution)/shard_map/all_to_all | solution.py:63
  369.2 0.1 copy.11
  369.3 0.9 copy.12
  (10 shorter events, 0.1 us)
Async XLA Ops:
  11.1 17.0 %copy-start.1 = (s32[48]{0:T(128)S(1)}, s32[48]{0:T(128)}, u32[]{:S(2)}) copy-start(s32[48]{0:T(128)} %param.6) | copy-start | bytes 580
  11.1 248.8 %all-to-all-start = ((bf16[32,2,320,128]{3,2,1,0:T(8,128)(2,1)}), bf16[32,2,320,128]{3,2,1,0:T(8,128)(2,1)}, u32[]{:S(2)}, u32[]{:S(2)}) async-start(bf16[32,2,320,128]{3,2,1,0:T(8,128)(2,1)} %stack.2), calls=%async_computation | async-start | bytes 10485760 | tf_op jit(solution)/shard_map/all_to_all | solution.py:10
  28.0 288.8 %all-gather.3.cloned.1.call-start = ((), (), s32[]{:S(2)}) async-start(), calls=%async_computation.2 | async-start | bytes 2088960 | tf_op jit(solution)/shard_map/all_gather | solution.py:33
  262.2 60.5 %copy-start.2 = (s32[1,4]{1,0:T(1,128)S(1)}, s32[1,4]{1,0:T(1,128)}, u32[]{:S(2)}) copy-start(s32[1,4]{1,0:T(1,128)} %param.7) | copy-start | bytes 52
  316.8 10.3 %copy-start = (bf16[7680,128]{1,0:T(8,128)(2,1)S(1)}, bf16[7680,128]{1,0:T(8,128)(2,1)}, u32[]{:S(2)}) copy-start(bf16[7680,128]{1,0:T(8,128)(2,1)} %all-gather.3.cloned.1.call-done) | copy-start | bytes 5898244
  319.4 4.4 %collective-permute-start = (f32[384,128]{1,0:T(8,128)S(1)}, f32[384,128]{1,0:T(8,128)S(1)}, u32[]{:S(2)}, u32[]{:S(2)}) collective-permute-start(f32[384,128]{1,0:T(8,128)S(1)} %fusion.4), channel_id=1, source_target_pairs={{0,1},{1,0},{2,3},{3,2},{4,5},{5,4},{6,7},{7,6},{8,9},{9,8},{10,11... | collective-permute-start | bytes 589832 | tf_op jit(solution)/shard_map/ppermute | solution.py:41
  323.8 5.9 %collective-permute-start.1 = (bf16[384,128]{1,0:T(8,128)(2,1)S(1)}, bf16[384,128]{1,0:T(8,128)(2,1)S(1)}, u32[]{:S(2)}, u32[]{:S(2)}) collective-permute-start(bf16[384,128]{1,0:T(8,128)(2,1)S(1)} %add_convert_fusion), channel_id=1, source_target_pairs={{0,2},{1,3},{2,0},{3,1},{4,6},{5,7},{6,4},{7,5},{8,10},{9,11},{10,... | collective-permute-start | bytes 294920 | tf_op jit(solution)/shard_map/ppermute | solution.py:43
Sparse Core Ops, SparseCore 0:
  262.3 54.4 all-gather.2
